TPU v7x, 32 devices: a whole 2x2x4 slice. The times are simulated.
32 devices in a mesh: tp: 4 (over y, core), dp: 8 (over z, x).
Axes of the slice: x: 2, y: 2, z: 4, core: 2. Of those that a mesh axis runs over, the one named last changes fastest.
Arguments:
- tokens: bfloat16 [24, 1024, 768], P('dp', 'tp'), may hold values from -6 to 6
- lengths: int32 [24], P('dp'), may hold values from 196 to 1024, as said below
- ln_gain: float32 [768], replicated, may hold values from 0.1 to 1.9
- w_qkv: bfloat16 [768, 2304], P(None, 'tp'), may hold values from -0.21875 to 0.21875
- q_gain: float32 [12, 64], P('tp'), may hold values from 0.1 to 1.9
- k_gain: float32 [12, 64], P('tp'), may hold values from 0.1 to 1.9
- w_proj: bfloat16 [768, 768], P('tp'), may hold values from -1.75 to 1.75
- w_fc1: bfloat16 [768, 3072], P(None, 'tp'), may hold values from -0.21875 to 0.21875
- b_fc1: float32 [3072], P('tp'), may hold values from -3 to 3
- w_fc2: bfloat16 [3072, 768], P('tp'), may hold values from -0.109375 to 0.109375
- b_fc2: float32 [768], replicated, may hold values from -2 to 2
- d_out: bfloat16 [24, 1024, 768], P('dp', 'tp'), may hold values from -6 to 6
Outputs:
- output: bfloat16 [24, 1024, 768], P('dp', 'tp')
- d_tokens: float32 [24, 1024, 768], P('dp', 'tp')
- d_ln_gain: float32 [768], replicated
- d_qkv: float32 [768, 2304], P(None, 'tp')
- d_q_gain: float32 [12, 64], P('tp')
- d_k_gain: float32 [12, 64], P('tp')
- d_proj: float32 [768, 768], P('tp')
- d_fc1: float32 [768, 3072], P(None, 'tp')
- d_bias_one: float32 [3072], P('tp')
- d_fc2: float32 [3072, 768], P('tp')
- d_bias_two: float32 [768], replicated
Inputs may be any that keep to these rules, and one draw needn't show every extreme that they name: `lengths`: each image's length is one of 196, 576 and 1024; every draw holds all three.
All inputs are finite; a program needn't handle non-finite values.
Results may differ from a plain program's by a relative error of at most 0.014.
Values may be sent and summed in bfloat16 or wider, within the bound.
No kernel may reach another device: no remote copies, remote signals or barrier semaphores. Data moves between devices by JAX's collectives and lax.ppermute only.
A program may use at most 192 MiB of HBM per device.

v0:
```python
import jax
import jax.numpy as jnp
from jax import lax
from jax.sharding import PartitionSpec as P

epsilon = 1e-06
masked_value = -1e30


def layer_norm(values, scale_gain):
    average = jnp.mean(values, axis=-1, keepdims=True)
    centred = values - average
    variance = jnp.mean(centred * centred, axis=-1, keepdims=True)
    return centred * lax.rsqrt(variance + epsilon) * scale_gain


def gelu_exact(values):
    return jax.nn.gelu(values, approximate=False)


def score_block(queries, keys_normed, length, factor):
    scores = (
        jnp.einsum("qhd,khd->hqk", queries, keys_normed, preferred_element_type=jnp.float32)
        * factor
    )
    visible = lax.broadcasted_iota(jnp.int32, scores.shape, 2) < length
    return (scores, visible)


def forward_keys(factor, operands):
    queries, keys_normed, value_rows, length = operands
    scores, visible = score_block(queries, keys_normed, length, factor)
    masked = jnp.where(visible, scores, masked_value)
    row_peak = jnp.max(masked, axis=-1, keepdims=True)
    exponent = jnp.exp(masked - row_peak)
    row_total = jnp.sum(exponent, axis=-1, keepdims=True)
    probability = (exponent / row_total).astype(jnp.bfloat16)
    attended = jnp.einsum(
        "hqk,khd->qhd", probability, value_rows, preferred_element_type=jnp.float32
    )
    return (attended, row_peak[..., 0] + jnp.log(row_total[..., 0]))


def backward_keys(factor, operands):
    queries, keys_normed, value_rows, d_attended, logsum, length = operands
    scores, visible = score_block(queries, keys_normed, length, factor)
    probability = jnp.where(visible, jnp.exp(scores - logsum[..., None]), 0.0)
    d_probs = jnp.einsum("qhd,khd->hqk", d_attended, value_rows, preferred_element_type=jnp.float32)
    row_dot = jnp.sum(probability * d_probs, axis=-1, keepdims=True)
    d_scores = (probability * (d_probs - row_dot)).astype(jnp.bfloat16)
    d_queries = (
        jnp.einsum("hqk,khd->qhd", d_scores, keys_normed, preferred_element_type=jnp.float32)
        * factor
    )
    d_keys = (
        jnp.einsum("hqk,qhd->khd", d_scores, queries, preferred_element_type=jnp.float32) * factor
    )
    d_values = jnp.einsum(
        "hqk,qhd->khd",
        probability.astype(jnp.bfloat16),
        d_attended,
        preferred_element_type=jnp.float32,
    )
    return (d_queries, d_keys, d_values)


def shards(
    tokens, lengths, ln_gain, w_qkv, q_gain, k_gain, w_proj, w_fc1, b_fc1, w_fc2, b_fc2, d_out
):
    images = tokens.shape[0]
    heads_here = q_gain.shape[0]
    head_size = q_gain.shape[1]
    factor = head_size ** (-0.5)
    tokens_float = tokens.astype(jnp.float32)
    normed_local = layer_norm(tokens_float, ln_gain).astype(jnp.bfloat16)
    normed = lax.all_gather(normed_local, "tp", axis=1, tiled=True)
    seq_len = normed.shape[1]
    joined = jnp.einsum("bsd,dc->bsc", normed, w_qkv, preferred_element_type=jnp.float32)
    split_heads = joined.reshape(images, seq_len, heads_here, 3, head_size)
    query_raw = split_heads[:, :, :, 0]
    key_raw = split_heads[:, :, :, 1]
    queries = layer_norm(query_raw, q_gain).astype(jnp.bfloat16)
    keys_normed = layer_norm(key_raw, k_gain).astype(jnp.bfloat16)
    value_rows = split_heads[:, :, :, 2].astype(jnp.bfloat16)

    def attend_image(operands):
        return forward_keys(factor, operands)

    attended, logsum = lax.map(attend_image, (queries, keys_normed, value_rows, lengths))
    attended = attended.reshape(images, seq_len, heads_here * head_size).astype(jnp.bfloat16)
    hidden = jnp.einsum("bsd,df->bsf", normed, w_fc1, preferred_element_type=jnp.float32) + b_fc1
    active = gelu_exact(hidden).astype(jnp.bfloat16)
    partial_sum = jnp.einsum("bsc,cd->bsd", attended, w_proj, preferred_element_type=jnp.float32)
    partial_sum = partial_sum + jnp.einsum(
        "bsf,fd->bsd", active, w_fc2, preferred_element_type=jnp.float32
    )
    summed = lax.psum_scatter(
        partial_sum.astype(jnp.bfloat16), "tp", scatter_dimension=1, tiled=True
    ).astype(jnp.float32)
    output = (tokens_float + summed + b_fc2).astype(jnp.bfloat16)
    d_rows = lax.all_gather(d_out, "tp", axis=1, tiled=True)
    d_fc2 = jnp.einsum("bsf,bsd->fd", active, d_rows, preferred_element_type=jnp.float32)
    d_proj = jnp.einsum("bsc,bsd->cd", attended, d_rows, preferred_element_type=jnp.float32)
    d_active = jnp.einsum("bsd,fd->bsf", d_rows, w_fc2, preferred_element_type=jnp.float32)
    _, gelu_back = jax.vjp(gelu_exact, hidden)
    d_hidden = gelu_back(d_active)[0].astype(jnp.bfloat16)
    d_fc1 = jnp.einsum("bsd,bsf->df", normed, d_hidden, preferred_element_type=jnp.float32)
    d_bias_one = jnp.sum(d_hidden, axis=(0, 1), dtype=jnp.float32)
    d_normed = jnp.einsum("bsf,df->bsd", d_hidden, w_fc1, preferred_element_type=jnp.float32)
    d_attended = jnp.einsum(
        "bsd,cd->bsc", d_rows, w_proj, preferred_element_type=jnp.float32
    ).astype(jnp.bfloat16)
    d_heads = d_attended.reshape(images, seq_len, heads_here, head_size)

    def back_image(operands):
        return backward_keys(factor, operands)

    d_queries, d_keys, d_values = lax.map(
        back_image, (queries, keys_normed, value_rows, d_heads, logsum, lengths)
    )
    _, query_back = jax.vjp(layer_norm, query_raw, q_gain)
    d_query_raw, d_q_gain = query_back(d_queries)
    _, key_back = jax.vjp(layer_norm, key_raw, k_gain)
    d_key_raw, d_k_gain = key_back(d_keys)
    d_joined = (
        jnp.stack([d_query_raw, d_key_raw, d_values], axis=3)
        .reshape(images, seq_len, -1)
        .astype(jnp.bfloat16)
    )
    d_qkv = jnp.einsum("bsd,bsc->dc", normed, d_joined, preferred_element_type=jnp.float32)
    d_normed = d_normed + jnp.einsum(
        "bsc,dc->bsd", d_joined, w_qkv, preferred_element_type=jnp.float32
    )
    d_local = lax.psum_scatter(
        d_normed.astype(jnp.bfloat16), "tp", scatter_dimension=1, tiled=True
    ).astype(jnp.float32)
    _, norm_back = jax.vjp(layer_norm, tokens_float, ln_gain)
    d_tokens_part, d_ln_gain = norm_back(d_local)
    d_tokens = d_out.astype(jnp.float32) + d_tokens_part
    d_bias_two = jnp.sum(d_out, axis=(0, 1), dtype=jnp.float32)
    d_ln_gain, d_bias_two = lax.psum((d_ln_gain, d_bias_two), ("tp", "dp"))
    d_qkv, d_q_gain, d_k_gain, d_proj, d_fc1, d_bias_one, d_fc2 = (
        lax.psum(d_qkv.astype(jnp.bfloat16), "dp").astype(jnp.float32),
        lax.psum(d_q_gain.astype(jnp.bfloat16), "dp").astype(jnp.float32),
        lax.psum(d_k_gain.astype(jnp.bfloat16), "dp").astype(jnp.float32),
        lax.psum(d_proj.astype(jnp.bfloat16), "dp").astype(jnp.float32),
        lax.psum(d_fc1.astype(jnp.bfloat16), "dp").astype(jnp.float32),
        lax.psum(d_bias_one.astype(jnp.bfloat16), "dp").astype(jnp.float32),
        lax.psum(d_fc2.astype(jnp.bfloat16), "dp").astype(jnp.float32),
    )
    return (
        output,
        d_tokens,
        d_ln_gain,
        d_qkv,
        d_q_gain,
        d_k_gain,
        d_proj,
        d_fc1,
        d_bias_one,
        d_fc2,
        d_bias_two,
    )


def solution(mesh):
    placed = (
        P("dp", "tp", None),
        P("dp"),
        P(),
        P(None, "tp"),
        P("tp", None),
        P("tp", None),
        P("tp", None),
        P(None, "tp"),
        P("tp"),
        P("tp", None),
        P(),
        P("dp", "tp", None),
    )
    return jax.shard_map(
        shards,
        mesh=mesh,
        in_specs=placed,
        out_specs=(
            P("dp", "tp", None),
            P("dp", "tp", None),
            P(),
            P(None, "tp"),
            P("tp", None),
            P("tp", None),
            P("tp", None),
            P(None, "tp"),
            P("tp"),
            P("tp", None),
            P(),
        ),
        check_vma=False,
    )
```

profile of v0, /device:TPU:0, one launch (start us, length us, event | category | flops | bytes accessed | tf_op | source)
XLA Modules:
  0.0 569.2 jit_solution(9019446906122960374)
XLA Ops:
  7.3 1.6 convert_reduce_fusion
  8.9 1.7 fusion.67
  11.9 1.4 fusion.65
  14.1 1.2 fusion.97
  15.3 2.4 copy.83
  17.7 36.0 %all-gather.3.cloned.1.call-done = bf16[3,1024,768]{2,1,0:T(8,128)(2,1)} async-done(((bf16[3,256,768]{2,1,0:T(8,128)(2,1)}), bf16[3,1024,768]{2,1,0:T(8,128)(2,1)}) %all-gather.3.cloned.1.call-update) | async-done | bytes 4718608 | tf_op jit(solution)/shard_map/all_gather | solution.py:76
  53.6 4.8 fusion.86
  59.2 1.3 fusion.77
  64.5 37.1 %while.28 = (s32[]{:T(128)}, bf16[3,1024,3,64]{1,3,2,0:T(8,128)(2,1)}, f32[3,3,1024]{2,1,0:T(4,128)}, bf16[3,1024,3,64]{1,3,2,0:T(8,128)(2,1)}, s32[3]{0:T(128)S...) while((s32[]{:T(128)}, bf16[3,1024,3,64]{1,3,2,0:T(8,128)(2,1)}, ...), condition=%wide.region_9.10_spmd.clone, body=%wide.region_6.9_spmd.sunk.clone | while | flops 843053056 | bytes 39823964 | solution.py:89
  65.8 2.4 fusion.151
  68.2 3.2 fusion.152
  72.0 4.9 fusion.153
  78.2 2.4 fusion.151
  80.5 3.2 fusion.152
  84.3 4.9 fusion.153
  90.5 2.4 fusion.151
  92.9 3.2 fusion.152
  96.7 4.9 fusion.153
  101.6 6.0 %convolution_convert_fusion = bf16[3,1024,192]{1,2,0:T(8,128)(2,1)} fusion(bf16[3,1024,768]{2,1,0:T(8,128)(2,1)} %all-gather.5.cloned.1.call-done, bf16[192,768]{1,0:T(8,128)(2,1)} %param.22), kind=kOutput, calls=%fused_computation.126 | convolution fusion | flops 906559488 | bytes 6193152 | tf_op jit(solution)/shard_map/bsd,cd->bsc/dot_general | solution.py:110
  107.6 87.6 %while.29 = (s32[]{:T(128)}, f32[3,1024,3,64]{1,3,2,0:T(8,128)}, f32[3,1024,3,64]{1,3,2,0:T(8,128)}, bf16[3,1024,3,64]{1,3,2,0:T(8,128)(2,1)}, bf16[3,1024,3,64]...) while((s32[]{:T(128)}, f32[3,1024,3,64]{1,3,2,0:T(8,128)}, ...), condition=%wide.region_13.14_spmd.clone, body=%wide.region_11.13_spmd.sunk.clone | while | flops 2060843008 | bytes 124744848 | solution.py:118
  107.8 3.1 fusion.162
  112.9 4.8 multiply_reduce_fusion.9
  117.7 5.6 multiply_convert_fusion.6
  123.3 6.0 %fusion.164 = f32[3,1024,3,64]{1,3,2,0:T(8,128)} fusion(f32[3,1024,3,64]{1,3,2,0:T(8,128)} %get-tuple-element.364, s32[]{:T(128)} %get-tuple-element.362, bf16[3,1024,1024]{1,2,0:T(8,128)(2,1)} %multiply_convert_fusion.6, bf16[3,1024,3,64]{1,3,2,0:T(8,128)(2,1)} %get-tuple-element.378), kind=kOutput, calls=%fused_computation.31.clone.1.clone | convolution fusion | flops 402849792 | bytes 7472128 | tf_op jit(solution)/shard_map/while/body/eval_jaxpr/hqk,qhd->khd/dot_general | solution.py:56
  129.3 3.1 fusion.163
  132.4 4.6 fusion.165
  137.0 2.9 fusion.162
  142.0 4.8 multiply_reduce_fusion.9
  146.8 5.6 multiply_convert_fusion.6
  152.4 6.0 %fusion.164 = f32[3,1024,3,64]{1,3,2,0:T(8,128)} fusion(f32[3,1024,3,64]{1,3,2,0:T(8,128)} %get-tuple-element.364, s32[]{:T(128)} %get-tuple-element.362, bf16[3,1024,1024]{1,2,0:T(8,128)(2,1)} %multiply_convert_fusion.6, bf16[3,1024,3,64]{1,3,2,0:T(8,128)(2,1)} %get-tuple-element.378), kind=kOutput, calls=%fused_computation.31.clone.1.clone | convolution fusion | flops 402849792 | bytes 7472128 | tf_op jit(solution)/shard_map/while/body/eval_jaxpr/hqk,qhd->khd/dot_general | solution.py:56
  158.4 3.1 fusion.163
  161.5 4.6 fusion.165
  166.1 2.9 fusion.162
  171.0 4.8 multiply_reduce_fusion.9
  175.8 5.6 multiply_convert_fusion.6
  181.5 6.0 %fusion.164 = f32[3,1024,3,64]{1,3,2,0:T(8,128)} fusion(f32[3,1024,3,64]{1,3,2,0:T(8,128)} %get-tuple-element.364, s32[]{:T(128)} %get-tuple-element.362, bf16[3,1024,1024]{1,2,0:T(8,128)(2,1)} %multiply_convert_fusion.6, bf16[3,1024,3,64]{1,3,2,0:T(8,128)(2,1)} %get-tuple-element.378), kind=kOutput, calls=%fused_computation.31.clone.1.clone | convolution fusion | flops 402849792 | bytes 7472128 | tf_op jit(solution)/shard_map/while/body/eval_jaxpr/hqk,qhd->khd/dot_general | solution.py:56
  187.5 3.1 fusion.163
  190.6 4.6 fusion.165
  195.2 2.5 multiply_reduce_fusion.4
  200.0 2.8 multiply_reduce_fusion.1
  204.4 1.9 pad_maximum_fusion
  207.1 6.4 %fusion.72 = (u8[1024,768]{1,0:T(8,128)(4,1)S(1)}, u8[1024,768]{1,0:T(8,128)(4,1)S(1)}, f32[3,1024,768]{2,1,0:T(8,128)S(1)}) fusion(f32[768]{0:T(1024)S(1)} %copy-done.43, bf16[3,1024,768]{2,1,0:T(8,128)(2,1)S(1)} %bitcast.228, bf16[768,768]{1,0:T(8,128)(2,1)S(1)} %copy-done), kind=kOutput, calls=%fused_computation.122 | convolution fusion | flops 3655335936 | bytes 16911360 | tf_op jit(solution)/shard_map/bsd,df->bsf/dot_general | solution.py:91
  213.5 23.0 %multiply_convert_fusion.1 = (bf16[3,1024,768]{2,1,0:T(8,128)(2,1)S(1)}, f32[3,1024,768]{2,1,0:T(8,128)}) fusion(f32[3,1024,768]{2,1,0:T(8,128)S(1)} %get-tuple-element.172, f32[768]{0:T(1024)S(1)} %copy-done.43, u8[1024,768]{1,0:T(8,128)(4,1)S(1)} %get-tuple-element.109, u8[1024,768]{1,0:T(8,128)(4,1)S(1)} %get-tuple-element.108), kind=kLoop, calls=%fused_computation.70 | loop fusion | flops 167510016 | bytes 25168896 | tf_op jit(solution)/shard_map/convert_element_type | solution.py:92
  236.5 7.9 %bitcast_convert_fusion.2 = bf16[768,576]{0,1:T(8,128)(2,1)} fusion(bf16[3,1024,576]{1,2,0:T(8,128)(2,1)S(1)} %bitcast.224, bf16[3,1024,768]{2,1,0:T(8,128)(2,1)} %all-gather.3.cloned.1.call-done), kind=kOutput, calls=%fused_computation.125 | convolution fusion | flops 2718351360 | bytes 9142272 | tf_op jit(solution)/shard_map/bsd,bsc->dc/dot_general | solution.py:130
  244.4 4.6 fusion.74
  249.0 14.2 %fusion.98 = (bf16[768]{0:T(1024)(128)(2,1)S(1)}, bf16[3,1024,768]{2,1,0:T(8,128)(2,1)}) fusion(f32[3,1024,768]{2,1,0:T(8,128)} %get-tuple-element.160, bf16[3,1024,768]{2,1,0:T(8,128)(2,1)} %all-gather.5.cloned.1.call-done, bf16[768,768]{1,0:T(8,128)(2,1)S(1)} %copy-done.44, f32[3,1024,768]{2,1,0:T(8,128)S(1)} %get-tuple-element.172, f32[768]{0:T(1024)S(1)} %copy-done.43), kind=kOutput, calls=%fused_computation.165 | convolution fusion | flops 3661626624 | bytes 29495808 | tf_op jit(solution)/shard_map/bsd,fd->bsf/dot_general | solution.py:104
  263.2 8.7 %bitcast_convert_fusion.1 = bf16[768,768]{1,0:T(8,128)(2,1)} fusion(bf16[3,1024,768]{2,1,0:T(8,128)(2,1)} %all-gather.3.cloned.1.call-done, bf16[3,1024,768]{2,1,0:T(8,128)(2,1)} %get-tuple-element.174), kind=kOutput, calls=%fused_computation.108 | convolution fusion | flops 3624468480 | bytes 10616832 | tf_op jit(solution)/shard_map/bsd,bsf->df/dot_general | solution.py:107
  271.9 7.3 %bitcast_convert_fusion = bf16[768,768]{1,0:T(8,128)(2,1)} fusion(bf16[3,1024,768]{2,1,0:T(8,128)(2,1)S(1)} %get-tuple-element.159, bf16[3,1024,768]{2,1,0:T(8,128)(2,1)} %all-gather.5.cloned.1.call-done), kind=kOutput, calls=%fused_computation.107 | convolution fusion | flops 3624468480 | bytes 10616832 | tf_op jit(solution)/shard_map/bsf,bsd->fd/dot_general | solution.py:102
  279.3 5.9 %fusion.81 = f32[3,1024,768]{2,1,0:T(8,128)S(1)} fusion(bf16[3,1024,768]{2,1,0:T(8,128)(2,1)} %get-tuple-element.174, bf16[768,768]{1,0:T(8,128)(2,1)S(1)} %copy-done), kind=kOutput, calls=%fused_computation.136 | convolution fusion | flops 3623878656 | bytes 15335424 | tf_op jit(solution)/shard_map/bsf,df->bsd/dot_general | solution.py:109
  285.3 5.6 add_convert_fusion
  291.0 6.1 %fusion.79 = f32[3,1024,768]{2,1,0:T(8,128)S(1)} fusion(bf16[3,1024,768]{2,1,0:T(8,128)(2,1)} %copy-done.13, bf16[768,768]{1,0:T(8,128)(2,1)S(1)} %copy-done.44), kind=kOutput, calls=%fused_computation.134 | convolution fusion | flops 3623878656 | bytes 15335424 | tf_op jit(solution)/shard_map/bsf,fd->bsd/dot_general | solution.py:94
  297.1 4.9 add_convert_fusion.2
  302.0 22.5 %all-reduce.1 = (bf16[3,64]{1,0:T(4,128)(2,1)S(1)}, bf16[3,64]{1,0:T(4,128)(2,1)S(1)}, bf16[768]{0:T(1024)(128)(2,1)S(1)}) all-reduce(bf16[3,64]{1,0:T(4,128)(2,1)S(1)} %get-tuple-element.176, bf16[3,64]{1,0:T(4,128)(2,1)S(1)} %get-tuple-element.110, bf16[768]{0:T(1024)(128)(2,1)S(1)} %get-tuple-element.173), channel_id=1, replica_groups=mesh['tp'=4,'dp'=8] {'dp'}, use_global_device_ids=true, to_apply=%region_25.26 | all-reduce | flops 1152 | bytes 4608 | tf_op jit(solution)/shard_map/psum | solution.py:144
  326.3 92.2 %all-reduce.5.cloned.1.call-done = (bf16[768,576]{0,1:T(8,128)(2,1)}, bf16[192,768]{1,0:T(8,128)(2,1)}, bf16[768,768]{1,0:T(8,128)(2,1)}, bf16[768,768]{1,0:T(8,128)(2,1)}) async-done(((bf16[768,576]{0,1:T(8,128)(2,1)}, bf16[192,768]{1,0:T(8,128)(2,1)}, bf16[768,768]{1,0:T(8,128)(2,1)}, bf16[768,768]{1,0:T(8,128)(2,1)}), (bf16[768,576]{0,1:T(8,128)(2,1)}, bf16[192,768]{1,0:T(8,128)(2,1)}, ...) | async-done | bytes 3538960 | tf_op jit(solution)/shard_map/psum | solution.py:143
  418.5 2.9 convert_element_type.130
  421.5 1.6 convert_element_type.133
  423.1 1.3 convert_element_type.122
  424.4 0.9 convert_element_type.128
  425.3 42.6 %reduce-scatter.5.cloned.1.call-done = bf16[3,256,768]{2,1,0:T(8,128)(2,1)} async-done(((bf16[3,1024,768]{2,1,0:T(8,128)(2,1)}), bf16[3,256,768]{2,1,0:T(8,128)(2,1)}) %reduce-scatter.5.cloned.1.call-update) | async-done | bytes 1179664 | tf_op jit(solution)/shard_map/reduce_scatter | solution.py:134
  467.8 2.0 fusion.68
  470.6 1.9 fusion.66
  473.1 45.0 %reduce-scatter.3.cloned.1.call-done = bf16[3,256,768]{2,1,0:T(8,128)(2,1)} async-done(((bf16[3,1024,768]{2,1,0:T(8,128)(2,1)}), bf16[3,256,768]{2,1,0:T(8,128)(2,1)}) %reduce-scatter.3.cloned.1.call-update) | async-done | bytes 1179664 | tf_op jit(solution)/shard_map/reduce_scatter | solution.py:97
  518.1 4.5 convert_reduce_fusion.1
  522.6 39.6 %all-reduce = (f32[768]{0:T(1024)}, f32[768]{0:T(1024)}) all-reduce(f32[768]{0:T(1024)} %get-tuple-element.114, f32[768]{0:T(1024)} %get-tuple-element.169), channel_id=1, replica_groups=mesh['tp'=4,'dp'=8] {'tp','dp'}, use_global_device_ids=true, to_apply=%region_22.23 | all-reduce | flops 1536 | bytes 12288 | tf_op jit(solution)/shard_map/psum | solution.py:141
  (163 shorter events, 25.8 us)
Async XLA Ops:
  7.2 199.6 %copy-start = (bf16[768,768]{1,0:T(8,128)(2,1)S(1)}, bf16[768,768]{1,0:T(8,128)(2,1)}, u32[]{:S(2)}) copy-start(bf16[768,768]{1,0:T(8,128)(2,1)} %param.23) | copy-start | bytes 3538948
  7.2 4.7 copy-start.6
  7.2 4.7 copy-start.34
  7.2 46.4 %all-gather.3.cloned.1.call-start = ((), (), s32[]{:S(2)}) async-start(), calls=%async_computation.2 | async-start | bytes 5898240 | tf_op jit(solution)/shard_map/all_gather | solution.py:76
  8.9 2.4 copy-start.32
  10.7 0.6 copy-start.38
  11.3 0.6 copy-start.36
  13.3 40.3 %copy-start.45 = (bf16[768,576]{0,1:T(8,128)(2,1)S(1)}, bf16[768,576]{0,1:T(8,128)(2,1)}, u32[]{:S(2)}) copy-start(bf16[768,576]{0,1:T(8,128)(2,1)} %param.19) | copy-start | bytes 2654212
  13.3 88.3 %all-gather.5.cloned.1.call-start = ((), (), s32[]{:S(2)}) async-start(), calls=%async_computation.4 | async-start | bytes 5898240 | tf_op jit(solution)/shard_map/all_gather | solution.py:101
  14.1 404.4 %all-reduce.5.cloned.1.call-start = ((), (), s32[]{:S(2)}) async-start(), calls=%async_computation.6 | async-start | bytes 7077888 | tf_op jit(solution)/shard_map/psum | solution.py:143
  59.2 4.0 copy-start.2
  59.2 4.5 copy-start.4
  60.9 2.3 copy-start.16
  61.3 0.6 copy-start.26
  61.3 1.9 copy-start.22
  61.9 1.4 copy-start.41
  62.2 1.5 copy-start.18
  62.6 0.6 copy-start.28
  63.2 0.7 copy-start.39
  63.2 1.1 copy-start.24
  63.9 0.7 copy-start.47
  101.6 6.0 %copy-start.8 = (bf16[3,1024,3,64]{1,3,2,0:T(8,128)(2,1)}, bf16[3,1024,3,64]{1,3,2,0:T(8,128)(2,1)S(1)}, u32[]{:S(2)}) copy-start(bf16[3,1024,3,64]{1,3,2,0:T(8,128)(2,1)S(1)} %get-tuple-element.394) | copy-start | bytes 3538948
  101.6 6.0 %copy-start.9 = (bf16[3,1024,3,64]{1,3,2,0:T(8,128)(2,1)}, bf16[3,1024,3,64]{1,3,2,0:T(8,128)(2,1)S(1)}, u32[]{:S(2)}) copy-start(bf16[3,1024,3,64]{1,3,2,0:T(8,128)(2,1)S(1)} %get-tuple-element.395) | copy-start | bytes 3538948
  107.6 87.6 %copy-start.5 = (f32[3,1024,3,1,64]{1,4,3,2,0:T(8,128)S(1)}, f32[3,1024,3,1,64]{1,4,3,2,0:T(8,128)}, u32[]{:S(2)}) copy-start(f32[3,1024,3,1,64]{1,4,3,2,0:T(8,128)} %copy-done.4) | copy-start | bytes 7077892
  107.6 87.6 %copy-start.40 = (f32[3,64]{1,0:T(4,128)S(1)}, f32[3,64]{1,0:T(4,128)}, u32[]{:S(2)}) copy-start(f32[3,64]{1,0:T(4,128)} %param.20) | copy-start | bytes 2308
  123.3 6.0 %copy-start.1 = (bf16[3,1024,1024]{1,2,0:T(8,128)(2,1)S(1)}, bf16[3,1024,1024]{1,2,0:T(8,128)(2,1)}, u32[]{:S(2)}) copy-start(bf16[3,1024,1024]{1,2,0:T(8,128)(2,1)} %multiply_convert_fusion.6) | copy-start | bytes 18874372 | tf_op jit(solution)/shard_map/while
  152.4 6.0 %copy-start.1 = (bf16[3,1024,1024]{1,2,0:T(8,128)(2,1)S(1)}, bf16[3,1024,1024]{1,2,0:T(8,128)(2,1)}, u32[]{:S(2)}) copy-start(bf16[3,1024,1024]{1,2,0:T(8,128)(2,1)} %multiply_convert_fusion.6) | copy-start | bytes 18874372 | tf_op jit(solution)/shard_map/while
  181.5 6.0 %copy-start.1 = (bf16[3,1024,1024]{1,2,0:T(8,128)(2,1)S(1)}, bf16[3,1024,1024]{1,2,0:T(8,128)(2,1)}, u32[]{:S(2)}) copy-start(bf16[3,1024,1024]{1,2,0:T(8,128)(2,1)} %multiply_convert_fusion.6) | copy-start | bytes 18874372 | tf_op jit(solution)/shard_map/while
  195.2 2.6 copy-start.29
  195.2 2.6 copy-start.3
  195.2 3.1 copy-start.11
  195.2 3.1 copy-start.17
  195.2 3.1 copy-start.42
  198.3 0.8 copy-start.27
  198.3 1.7 copy-start.10
  198.3 1.7 copy-start.19
  198.3 1.7 copy-start.23
  198.4 1.7 copy-start.25
  203.6 3.1 slice-start
  204.4 2.3 slice-start.1
  206.4 0.7 copy-start.43
  207.1 29.4 %copy-start.14 = (bf16[3,1024,3,3,64]{1,4,3,2,0:T(8,128)(2,1)}, bf16[3,1024,3,3,64]{1,4,3,2,0:T(8,128)(2,1)S(1)}, u32[]{:S(2)}) copy-start(bf16[3,1024,3,3,64]{1,4,3,2,0:T(8,128)(2,1)S(1)} %copy.30) | copy-start | bytes 10616836
  236.5 35.4 %copy-start.13 = (bf16[3,1024,768]{2,1,0:T(8,128)(2,1)}, bf16[3,1024,768]{2,1,0:T(8,128)(2,1)S(1)}, u32[]{:S(2)}) copy-start(bf16[3,1024,768]{2,1,0:T(8,128)(2,1)S(1)} %get-tuple-element.159) | copy-start | bytes 14155780
  244.4 4.6 copy-start.44
  279.2 6.0 %copy-start.46 = (bf16[768,576]{0,1:T(8,128)(2,1)S(1)}, bf16[768,576]{0,1:T(8,128)(2,1)}, u32[]{:S(2)}) copy-start(bf16[768,576]{0,1:T(8,128)(2,1)} %param.19) | copy-start | bytes 2654212
  279.3 188.6 %reduce-scatter.5.cloned.1.call-start = ((), (), s32[]{:S(2)}) async-start(), calls=%async_computation.5 | async-start | bytes 5898240 | tf_op jit(solution)/shard_map/reduce_scatter | solution.py:134
  279.3 6.0 %copy-start.15 = (bf16[3,1024,3,3,64]{1,4,3,2,0:T(8,128)(2,1)S(1)}, bf16[3,1024,3,3,64]{1,4,3,2,0:T(8,128)(2,1)}, u32[]{:S(2)}) copy-start(bf16[3,1024,3,3,64]{1,4,3,2,0:T(8,128)(2,1)} %copy-done.14) | copy-start | bytes 10616836
  290.9 6.1 %copy-start.31 = (bf16[192,768]{1,0:T(8,128)(2,1)S(1)}, bf16[192,768]{1,0:T(8,128)(2,1)}, u32[]{:S(2)}) copy-start(bf16[192,768]{1,0:T(8,128)(2,1)} %param.22) | copy-start | bytes 884740
  291.0 227.1 %reduce-scatter.3.cloned.1.call-start = ((), (), s32[]{:S(2)}) async-start(), calls=%async_computation.3 | async-start | bytes 5898240 | tf_op jit(solution)/shard_map/reduce_scatter | solution.py:97
  418.5 2.9 copy-start.20
  421.5 1.6 copy-start.21
  421.5 2.9 copy-start.30
  423.0 44.8 %copy-start.7 = (bf16[3,256,768]{2,1,0:T(8,128)(2,1)S(1)}, bf16[3,256,768]{2,1,0:T(8,128)(2,1)}, u32[]{:S(2)}) copy-start(bf16[3,256,768]{2,1,0:T(8,128)(2,1)} %param.16) | copy-start | bytes 3538948
  423.0 44.8 %copy-start.33 = (f32[3,256]{1,0:T(4,128)S(1)}, f32[3,256]{1,0:T(4,128)}, u32[]{:S(2)}) copy-start(f32[3,256]{1,0:T(4,128)} %copy-done.32) | copy-start | bytes 9220
  423.1 44.8 %copy-start.35 = (f32[768]{0:T(1024)S(1)}, f32[768]{0:T(1024)}, u32[]{:S(2)}) copy-start(f32[768]{0:T(1024)} %param.18) | copy-start | bytes 9220
  423.1 47.5 %copy-start.37 = (f32[3,256]{1,0:T(4,128)S(1)}, f32[3,256]{1,0:T(4,128)}, u32[]{:S(2)}) copy-start(f32[3,256]{1,0:T(4,128)} %copy-done.36) | copy-start | bytes 9220
  467.8 2.7 copy-start.12
Sparse Core Ops, SparseCore 0:
  13.5 40.1 all-gather.2
  55.2 37.4 all-gather.4
  279.4 139.1 all-reduce.4
  420.9 46.8 reduce-scatter.4
  470.2 47.8 reduce-scatter.2
where the time goes:
time: 580 us; the launch traced here: 569 us
  waiting for transfers between devices  216 us (37%)
  matrix products  169 us (29%)
  other arithmetic  91.3 us (16%)
  blocking collectives  62.1 us (11%)
  local copies, waits for them, and re-layouts  15.1 us (3%)
  between operations  14.8 us (3%)
    psum x1, waiting for transfers between devices, shards(): lax.psum(d_qkv.astype(jnp.bfloat16), 'dp').astype(jnp.float32)  92.2 us
    reduce_scatter x1, waiting for transfers between devices, shards(): lax.psum_scatter(partial_sum.astype(jnp.bfloat16), 'tp', scatter_dimensio...  45 us
    reduce_scatter x1, waiting for transfers between devices, shards(): lax.psum_scatter(d_normed.astype(jnp.bfloat16), 'tp', scatter_dimension=1...  42.6 us
    psum x1, blocking collectives, shards(): d_ln_gain, d_bias_two = lax.psum((d_ln_gain, d_bias_two), ('tp', 'dp'))  39.6 us
    all_gather x1, waiting for transfers between devices, shards(): normed = lax.all_gather(normed_local, 'tp', axis=1, tiled=True)  36 us
    convert_element_type x1, other arithmetic, shards(): active = gelu_exact(hidden).astype(jnp.bfloat16)  23 us
    psum x1, blocking collectives, shards(): lax.psum(d_q_gain.astype(jnp.bfloat16), 'dp').astype(jnp.float32)  22.5 us
    dot_general x3, matrix products, backward_keys(): jnp.einsum('hqk,qhd->khd', d_scores, queries, preferred_element_type=jnp....  17.9 us
  transfers between devices with their start and end apart: 5, of which 4 were waited for; matrix products, arithmetic and copies ran while one was open for 15% of the time, Pallas kernels for 0%

commit v1 on v0

--- a/solution.py
+++ b/solution.py
@@ -1,3 +1,4 @@
+import functools
 import jax
 import jax.numpy as jnp
 from jax import lax
@@ -5,6 +6,23 @@
 
 epsilon = 1e-06
 masked_value = -1e30
+
+
+def track_skins(my_data, comm_axis, d0):
+    carry_in = lax.axis_size(comm_axis)
+    side_arr = lax.axis_index(comm_axis)
+    next_value, passed, all_values = (carry_in, side_arr, my_data.shape[d0])
+    y1, work_now = (my_data, 1)
+    while work_now < next_value:
+        after = tuple(((it, (it - work_now) % next_value) for it in range(next_value)))
+        reached = lax.ppermute(y1, axis_name=comm_axis, perm=after)
+        y1 = jnp.concatenate([y1, reached], d0)
+        work_now = 2 * work_now
+    w2 = jnp.roll(y1, passed * all_values, axis=d0)
+    return w2
+
+
+reach_numbers = functools.partial(track_skins, comm_axis="tp", d0=1)
 
 
 def layer_norm(values, scale_gain):
@@ -73,7 +91,7 @@
     factor = head_size ** (-0.5)
     tokens_float = tokens.astype(jnp.float32)
     normed_local = layer_norm(tokens_float, ln_gain).astype(jnp.bfloat16)
-    normed = lax.all_gather(normed_local, "tp", axis=1, tiled=True)
+    normed = reach_numbers(normed_local)
     seq_len = normed.shape[1]
     joined = jnp.einsum("bsd,dc->bsc", normed, w_qkv, preferred_element_type=jnp.float32)
     split_heads = joined.reshape(images, seq_len, heads_here, 3, head_size)

time: 580 us -> 650 us (1.12)
  waiting for transfers between devices: 216 us -> 268 us
  local copies, waits for them, and re-layouts: 15.1 us -> 26.8 us
    ppermute x0 -> x2, waiting for transfers between devices: none -> 88 us  [track_skins(): reached = lax.ppermute(y1, axis_name=comm_axis, perm=after)]
    all_gather x1 -> x0, waiting for transfers between devices: 36 us -> none  [shards(): normed = lax.all_gather(normed_local, 'tp', axis=1, tiled=True)]
    unnamed x99 -> x111, local copies, waits for them, and re-layouts: 7 us -> 15.2 us
  transfers between devices with their start and end apart: 5 -> 6, of which waited for: 4 -> 5; matrix products, arithmetic and copies ran while one was open for 15% -> 20% of each run, Pallas kernels for 0% -> 0%
where the time goes in v1:
time: 650 us; the launch traced here: 639 us
  waiting for transfers between devices  268 us (41%)
  matrix products  170 us (26%)
  other arithmetic  93.1 us (14%)
  blocking collectives  62.5 us (10%)
  local copies, waits for them, and re-layouts  26.8 us (4%)
  between operations  15 us (2%)
    psum x1, waiting for transfers between devices, shards(): lax.psum(d_qkv.astype(jnp.bfloat16), 'dp').astype(jnp.float32)  92.1 us
    ppermute x2, waiting for transfers between devices, track_skins(): reached = lax.ppermute(y1, axis_name=comm_axis, perm=after)  88 us
    reduce_scatter x1, waiting for transfers between devices, shards(): lax.psum_scatter(partial_sum.astype(jnp.bfloat16), 'tp', scatter_dimensio...  45 us
    reduce_scatter x1, waiting for transfers between devices, shards(): lax.psum_scatter(d_normed.astype(jnp.bfloat16), 'tp', scatter_dimension=1...  42.7 us
    psum x1, blocking collectives, shards(): d_ln_gain, d_bias_two = lax.psum((d_ln_gain, d_bias_two), ('tp', 'dp'))  39.6 us
    psum x1, blocking collectives, shards(): lax.psum(d_q_gain.astype(jnp.bfloat16), 'dp').astype(jnp.float32)  22.9 us
    convert_element_type x1, other arithmetic, shards(): active = gelu_exact(hidden).astype(jnp.bfloat16)  22.8 us
    dot_general x3, matrix products, backward_keys(): jnp.einsum('hqk,qhd->khd', d_scores, queries, preferred_element_type=jnp....  17.9 us
  transfers between devices with their start and end apart: 6, of which 5 were waited for; matrix products, arithmetic and copies ran while one was open for 20% of the time, Pallas kernels for 0%

profile of v1, /device:TPU:0, one launch (start us, length us, event | category | flops | bytes accessed | tf_op | source)
XLA Modules:
  0.0 639.0 jit_solution(5633780048686822125)
XLA Ops:
  7.2 1.6 convert_reduce_fusion
  8.9 1.7 fusion.75
  11.3 2.2 constant_dynamic-update-slice_fusion.5
  13.4 2.4 collective-permute-start
  15.9 13.7 %collective-permute-done = bf16[3,256,768]{2,1,0:T(8,128)(2,1)S(1)} collective-permute-done((bf16[3,256,768]{2,1,0:T(8,128)(2,1)S(1)}, bf16[3,256,768]{2,1,0:T(8,128)(2,1)S(1)}, u32[]{:S(2)}, u32[]{:S(2)}) %collective-permute-start) | collective-permute-done | bytes 1179680 | tf_op jit(solution)/shard_map/ppermute | solution.py:18
  33.0 2.4 copy.88
  36.5 74.2 %collective-permute-done.1 = bf16[3,512,768]{2,1,0:T(8,128)(2,1)} collective-permute-done((bf16[3,512,768]{2,1,0:T(8,128)(2,1)}, bf16[3,512,768]{2,1,0:T(8,128)(2,1)}, u32[]{:S(2)}, u32[]{:S(2)}) %collective-permute-start.1) | collective-permute-done | bytes 2359328 | tf_op jit(solution)/shard_map/ppermute | solution.py:18
  110.8 3.2 constant_dynamic-update-slice_fusion.3
  116.2 3.2 constant_dynamic-update-slice_fusion
  119.4 4.8 fusion.69
  129.8 37.1 %while.28 = (s32[]{:T(128)}, bf16[3,1024,3,64]{1,3,2,0:T(8,128)(2,1)}, f32[3,3,1024]{2,1,0:T(4,128)}, bf16[3,1024,3,64]{1,3,2,0:T(8,128)(2,1)}, s32[3]{0:T(128)S...) while((s32[]{:T(128)}, bf16[3,1024,3,64]{1,3,2,0:T(8,128)(2,1)}, ...), condition=%wide.region_9.10_spmd.clone, body=%wide.region_6.9_spmd.sunk.clone | while | flops 843053056 | bytes 39823964 | solution.py:107
  131.0 2.4 fusion.162
  133.4 3.2 fusion.163
  137.2 4.9 fusion.164
  143.4 2.4 fusion.162
  145.7 3.2 fusion.163
  149.5 4.9 fusion.164
  155.7 2.4 fusion.162
  158.1 3.2 fusion.163
  161.9 4.9 fusion.164
  166.9 9.1 %fusion.80 = (u8[1024,768]{1,0:T(8,128)(4,1)S(1)}, u8[1024,768]{1,0:T(8,128)(4,1)S(1)}, f32[3,1024,768]{2,1,0:T(8,128)S(1)}) fusion(f32[768]{0:T(1024)S(1)} %copy-done.43, bf16[768,768]{1,0:T(8,128)(2,1)S(1)} %copy-done, bf16[3,2048,768]{2,1,0:T(8,128)(2,1)} %constant_dynamic-update-slice_fusion, s32[]{:T(128)S(6)} %select_n.21), kind=kOutput, calls=%fused_computation.131 | convolution fusion | flops 3655335936 | bytes 16911364 | tf_op jit(solution)/shard_map/bsd,df->bsf/dot_general | solution.py:109
  176.0 3.7 copy-done.13
  179.6 22.8 %multiply_convert_fusion.1 = (bf16[3,1024,768]{2,1,0:T(8,128)(2,1)}, f32[3,1024,768]{2,1,0:T(8,128)}) fusion(f32[3,1024,768]{2,1,0:T(8,128)S(1)} %get-tuple-element.174, f32[768]{0:T(1024)S(1)} %copy-done.43, u8[1024,768]{1,0:T(8,128)(4,1)S(1)} %get-tuple-element.109, u8[1024,768]{1,0:T(8,128)(4,1)S(1)} %get-tuple-element.108), kind=kLoop, calls=%fused_computation.70 | loop fusion | flops 167510016 | bytes 25168896 | tf_op jit(solution)/shard_map/convert_element_type | solution.py:110
  202.5 5.0 convolution_convert_fusion
  207.5 87.7 %while.29 = (s32[]{:T(128)}, f32[3,1024,3,64]{1,3,2,0:T(8,128)}, f32[3,1024,3,64]{1,3,2,0:T(8,128)}, bf16[3,1024,3,64]{1,3,2,0:T(8,128)(2,1)}, bf16[3,1024,3,64]...) while((s32[]{:T(128)}, f32[3,1024,3,64]{1,3,2,0:T(8,128)}, ...), condition=%wide.region_13.14_spmd.clone, body=%wide.region_11.13_spmd.sunk.clone | while | flops 2060843008 | bytes 124744848 | solution.py:136
  207.5 3.1 fusion.173
  212.6 4.8 multiply_reduce_fusion.9
  217.4 5.7 multiply_convert_fusion.6
  223.2 6.0 fusion.175
  229.1 3.1 fusion.174
  232.2 4.6 fusion.176
  236.8 2.9 fusion.173
  241.8 4.8 multiply_reduce_fusion.9
  246.6 5.7 multiply_convert_fusion.6
  252.3 6.0 fusion.175
  258.3 3.1 fusion.174
  261.4 4.6 fusion.176
  266.0 2.9 fusion.173
  270.9 4.8 multiply_reduce_fusion.9
  275.8 5.7 multiply_convert_fusion.6
  281.5 6.0 fusion.175
  287.5 3.1 fusion.174
  290.6 4.6 fusion.176
  295.3 2.5 multiply_reduce_fusion.4
  299.6 2.6 multiply_reduce_fusion.1
  306.0 7.8 %bitcast_convert_fusion.2 = bf16[768,576]{0,1:T(8,128)(2,1)} fusion(bf16[3,1024,576]{1,2,0:T(8,128)(2,1)S(1)} %bitcast.224, bf16[3,2048,768]{2,1,0:T(8,128)(2,1)} %constant_dynamic-update-slice_fusion, s32[]{:T(128)S(6)} %select_n.21), kind=kOutput, calls=%fused_computation.134 | convolution fusion | flops 2718351360 | bytes 9142276 | tf_op jit(solution)/shard_map/bsd,bsc->dc/dot_general | solution.py:148
  313.8 14.2 %fusion.113 = (bf16[768]{0:T(1024)(128)(2,1)S(1)}, bf16[3,1024,768]{2,1,0:T(8,128)(2,1)}) fusion(f32[3,1024,768]{2,1,0:T(8,128)} %get-tuple-element.160, bf16[3,1024,768]{2,1,0:T(8,128)(2,1)} %all-gather.2.cloned.1.call-done, bf16[768,768]{1,0:T(8,128)(2,1)S(1)} %copy-done.45, f32[3,1024,768]{2,1,0:T(8,128)S(1)} %bitcast.219, f32[768]{0:T(1024)S(1)} %copy-done.44), kind=kOutput, calls=%fused_computation.182 | convolution fusion | flops 3661626624 | bytes 29495808 | tf_op jit(solution)/shard_map/bsd,fd->bsf/dot_general | solution.py:122
  328.0 8.7 %bitcast_convert_fusion.1 = bf16[768,768]{1,0:T(8,128)(2,1)} fusion(bf16[3,1024,768]{2,1,0:T(8,128)(2,1)} %get-tuple-element.176, bf16[3,2048,768]{2,1,0:T(8,128)(2,1)} %constant_dynamic-update-slice_fusion, s32[]{:T(128)S(6)} %select_n.21), kind=kOutput, calls=%fused_computation.117 | convolution fusion | flops 3624468480 | bytes 10616836 | tf_op jit(solution)/shard_map/bsd,bsf->df/dot_general | solution.py:125
  336.7 4.5 fusion.86
  341.2 7.3 %bitcast_convert_fusion = bf16[768,768]{1,0:T(8,128)(2,1)} fusion(bf16[3,1024,768]{2,1,0:T(8,128)(2,1)S(1)} %bitcast.223, bf16[3,1024,768]{2,1,0:T(8,128)(2,1)} %all-gather.2.cloned.1.call-done), kind=kOutput, calls=%fused_computation.116 | convolution fusion | flops 3624468480 | bytes 10616832 | tf_op jit(solution)/shard_map/bsf,bsd->fd/dot_general | solution.py:120
  348.6 5.9 fusion.93
  354.6 5.6 add_convert_fusion
  360.6 5.8 fusion.91
  366.4 5.0 add_convert_fusion.2
  371.4 22.9 %all-reduce.1 = (bf16[3,64]{1,0:T(4,128)(2,1)S(1)}, bf16[3,64]{1,0:T(4,128)(2,1)S(1)}, bf16[768]{0:T(1024)(128)(2,1)S(1)}) all-reduce(bf16[3,64]{1,0:T(4,128)(2,1)S(1)} %get-tuple-element.178, bf16[3,64]{1,0:T(4,128)(2,1)S(1)} %get-tuple-element.110, bf16[768]{0:T(1024)(128)(2,1)S(1)} %get-tuple-element.175), channel_id=1, replica_groups=mesh['tp'=4,'dp'=8] {'dp'}, use_global_device_ids=true, to_apply=%region_25.26 | all-reduce | flops 1152 | bytes 4608 | tf_op jit(solution)/shard_map/psum | solution.py:162
  396.0 92.1 %all-reduce.5.cloned.1.call-done = (bf16[768,576]{0,1:T(8,128)(2,1)}, bf16[192,768]{1,0:T(8,128)(2,1)}, bf16[768,768]{1,0:T(8,128)(2,1)}, bf16[768,768]{1,0:T(8,128)(2,1)}) async-done(((bf16[768,576]{0,1:T(8,128)(2,1)}, bf16[192,768]{1,0:T(8,128)(2,1)}, bf16[768,768]{1,0:T(8,128)(2,1)}, bf16[768,768]{1,0:T(8,128)(2,1)}), (bf16[768,576]{0,1:T(8,128)(2,1)}, bf16[192,768]{1,0:T(8,128)(2,1)}, ...) | async-done | bytes 3538960 | tf_op jit(solution)/shard_map/psum | solution.py:161
  488.2 3.0 convert_element_type.130
  491.2 1.6 convert_element_type.133
  495.0 42.7 %reduce-scatter.5.cloned.1.call-done = bf16[3,256,768]{2,1,0:T(8,128)(2,1)} async-done(((bf16[3,1024,768]{2,1,0:T(8,128)(2,1)}), bf16[3,256,768]{2,1,0:T(8,128)(2,1)}) %reduce-scatter.5.cloned.1.call-update) | async-done | bytes 1179664 | tf_op jit(solution)/shard_map/reduce_scatter | solution.py:152
  537.7 2.0 fusion.76
  540.4 1.9 fusion.74
  542.9 45.0 %reduce-scatter.3.cloned.1.call-done = bf16[3,256,768]{2,1,0:T(8,128)(2,1)} async-done(((bf16[3,1024,768]{2,1,0:T(8,128)(2,1)}), bf16[3,256,768]{2,1,0:T(8,128)(2,1)}) %reduce-scatter.3.cloned.1.call-update) | async-done | bytes 1179664 | tf_op jit(solution)/shard_map/reduce_scatter | solution.py:115
  587.9 4.5 convert_reduce_fusion.1
  592.4 39.6 %all-reduce = (f32[768]{0:T(1024)}, f32[768]{0:T(1024)}) all-reduce(f32[768]{0:T(1024)} %get-tuple-element.114, f32[768]{0:T(1024)} %get-tuple-element.171), channel_id=1, replica_groups=mesh['tp'=4,'dp'=8] {'tp','dp'}, use_global_device_ids=true, to_apply=%region_22.23 | all-reduce | flops 1536 | bytes 12288 | tf_op jit(solution)/shard_map/psum | solution.py:159
  (179 shorter events, 35.2 us)
Async XLA Ops:
  7.2 159.7 %copy-start = (bf16[768,768]{1,0:T(8,128)(2,1)S(1)}, bf16[768,768]{1,0:T(8,128)(2,1)}, u32[]{:S(2)}) copy-start(bf16[768,768]{1,0:T(8,128)(2,1)} %param.23) | copy-start | bytes 3538948
  7.2 4.1 copy-start.6
  7.2 195.3 %all-gather.2.cloned.1.call-start = ((), (), s32[]{:S(2)}) async-start(), calls=%async_computation.3 | async-start | bytes 5898240 | tf_op jit(solution)/shard_map/all_gather | solution.py:119
  8.9 4.5 copy-start.33
  10.7 0.6 copy-start.38
  11.3 4.6 copy-start.36
  13.4 16.2 %collective-permute-start = (bf16[3,256,768]{2,1,0:T(8,128)(2,1)S(1)}, bf16[3,256,768]{2,1,0:T(8,128)(2,1)S(1)}, u32[]{:S(2)}, u32[]{:S(2)}) collective-permute-start(bf16[3,256,768]{2,1,0:T(8,128)(2,1)S(1)} %get-tuple-element.162), channel_id=1, source_target_pairs={{0,24},{8,0},{16,8},{24,16},{1,25},{9,1},{17,9},{25,17},{2,26},{10... | collective-permute-start | bytes 3538952 | tf_op jit(solution)/shard_map/ppermute | solution.py:18
  31.2 79.6 %collective-permute-start.1 = (bf16[3,512,768]{2,1,0:T(8,128)(2,1)}, bf16[3,512,768]{2,1,0:T(8,128)(2,1)}, u32[]{:S(2)}, u32[]{:S(2)}) collective-permute-start(bf16[3,512,768]{2,1,0:T(8,128)(2,1)} %pad_maximum_fusion.1), channel_id=1, source_target_pairs={{0,16},{8,24},{16,0},{24,8},{1,17},{9,25},{17,1},{25,9},{2,18},{10... | collective-permute-start | bytes 7077896 | tf_op jit(solution)/shard_map/ppermute | solution.py:18
  31.8 456.4 %all-reduce.5.cloned.1.call-start = ((), (), s32[]{:S(2)}) async-start(), calls=%async_computation.5 | async-start | bytes 7077888 | tf_op jit(solution)/shard_map/psum | solution.py:161
  115.1 4.4 copy-start.46
  125.0 3.7 copy-start.4
  125.0 4.2 copy-start.2
  126.7 2.0 copy-start.18
  127.1 0.6 copy-start.26
  127.1 1.6 copy-start.39
  127.2 2.1 copy-start.24
  127.5 1.8 copy-start.41
  127.7 2.0 copy-start.16
  128.1 0.6 copy-start.28
  128.8 1.0 copy-start.22
  128.8 1.0 copy-start.48
  129.7 37.1 %copy-start.43 = (f32[768]{0:T(1024)S(1)}, f32[768]{0:T(1024)}, u32[]{:S(2)}) copy-start(f32[768]{0:T(1024)} %param.24) | copy-start | bytes 9220
  166.8 9.1 %copy-start.8 = (bf16[3,1024,3,64]{1,3,2,0:T(8,128)(2,1)}, bf16[3,1024,3,64]{1,3,2,0:T(8,128)(2,1)S(1)}, u32[]{:S(2)}) copy-start(bf16[3,1024,3,64]{1,3,2,0:T(8,128)(2,1)S(1)} %get-tuple-element.395) | copy-start | bytes 3538948
  166.8 9.1 %copy-start.9 = (bf16[3,1024,3,64]{1,3,2,0:T(8,128)(2,1)}, bf16[3,1024,3,64]{1,3,2,0:T(8,128)(2,1)S(1)}, u32[]{:S(2)}) copy-start(bf16[3,1024,3,64]{1,3,2,0:T(8,128)(2,1)S(1)} %get-tuple-element.396) | copy-start | bytes 3538948
  176.0 3.7 copy-start.13
  179.6 22.9 %copy-start.31 = (bf16[192,768]{1,0:T(8,128)(2,1)S(1)}, bf16[192,768]{1,0:T(8,128)(2,1)}, u32[]{:S(2)}) copy-start(bf16[192,768]{1,0:T(8,128)(2,1)} %param.22) | copy-start | bytes 884740
  207.5 87.7 %copy-start.5 = (f32[3,1024,3,1,64]{1,4,3,2,0:T(8,128)S(1)}, f32[3,1024,3,1,64]{1,4,3,2,0:T(8,128)}, u32[]{:S(2)}) copy-start(f32[3,1024,3,1,64]{1,4,3,2,0:T(8,128)} %copy-done.4) | copy-start | bytes 7077892
  207.5 87.7 %copy-start.40 = (f32[3,64]{1,0:T(4,128)S(1)}, f32[3,64]{1,0:T(4,128)}, u32[]{:S(2)}) copy-start(f32[3,64]{1,0:T(4,128)} %param.20) | copy-start | bytes 2308
  223.2 6.0 copy-start.1
  252.3 6.0 copy-start.1
  281.5 6.0 copy-start.1
  295.2 2.6 copy-start.27
  295.2 2.7 copy-start.3
  295.2 3.1 copy-start.11
  295.2 3.1 copy-start.17
  295.2 3.1 copy-start.42
  297.8 1.3 copy-start.29
  297.8 1.8 copy-start.10
  297.8 1.8 copy-start.19
  297.8 1.8 copy-start.23
  297.8 1.8 copy-start.25
  305.3 8.4 %slice-start = ((s8[9437184]{0:T(1024)(128)(4,1)}), s8[4194304]{0:T(1024)(128)(4,1)S(1)}, s32[]{:S(2)}) async-start(s8[9437184]{0:T(1024)(128)(4,1)} %bitcast.218), calls=%async_computation.6 | async-start | bytes 8388608
  305.9 7.8 %copy-start.14 = (bf16[3,1024,3,3,64]{1,4,3,2,0:T(8,128)(2,1)}, bf16[3,1024,3,3,64]{1,4,3,2,0:T(8,128)(2,1)S(1)}, u32[]{:S(2)}) copy-start(bf16[3,1024,3,3,64]{1,4,3,2,0:T(8,128)(2,1)S(1)} %copy.30) | copy-start | bytes 10616836
  305.9 7.8 %slice-start.1 = ((s8[9437184]{0:T(1024)(128)(4,1)}), s8[4194304]{0:T(1024)(128)(4,1)S(1)}, s32[]{:S(2)}) async-start(s8[9437184]{0:T(1024)(128)(4,1)} %bitcast.218), calls=%async_computation.7 | async-start | bytes 8388608
  305.9 7.8 %slice-start.2 = ((s8[9437184]{0:T(1024)(128)(4,1)}), s8[1048576]{0:T(1024)(128)(4,1)S(1)}, s32[]{:S(2)}) async-start(s8[9437184]{0:T(1024)(128)(4,1)} %bitcast.218), calls=%async_computation.8 | async-start | bytes 2097152
  305.9 7.8 %copy-start.44 = (f32[768]{0:T(1024)S(1)}, f32[768]{0:T(1024)}, u32[]{:S(2)}) copy-start(f32[768]{0:T(1024)} %param.24) | copy-start | bytes 9220
  305.9 7.8 %copy-start.45 = (bf16[768,768]{1,0:T(8,128)(2,1)S(1)}, bf16[768,768]{1,0:T(8,128)(2,1)}, u32[]{:S(2)}) copy-start(bf16[768,768]{1,0:T(8,128)(2,1)} %param.25) | copy-start | bytes 3538948
  305.9 35.3 %slice-start.3 = ((s8[4718592]{0:T(1024)(128)(4,1)}), s8[4194304]{0:T(1024)(128)(4,1)S(1)}, s32[]{:S(2)}) async-start(s8[4718592]{0:T(1024)(128)(4,1)} %bitcast.222), calls=%async_computation.9 | async-start | bytes 8388608
  313.8 27.4 %slice-start.4 = ((s8[4718592]{0:T(1024)(128)(4,1)}), s8[524288]{0:T(1024)(128)(4,1)S(1)}, s32[]{:S(2)}) async-start(s8[4718592]{0:T(1024)(128)(4,1)} %bitcast.222), calls=%async_computation.10 | async-start | bytes 1048576
  348.6 6.0 copy-start.47
  348.6 189.1 %reduce-scatter.5.cloned.1.call-start = ((), (), s32[]{:S(2)}) async-start(), calls=%async_computation.4 | async-start | bytes 5898240 | tf_op jit(solution)/shard_map/reduce_scatter | solution.py:152
  348.6 6.0 copy-start.15
  360.3 6.1 copy-start.32
  360.3 227.7 %reduce-scatter.3.cloned.1.call-start = ((), (), s32[]{:S(2)}) async-start(), calls=%async_computation.2 | async-start | bytes 5898240 | tf_op jit(solution)/shard_map/reduce_scatter | solution.py:115
  488.2 3.0 copy-start.20
  488.2 4.6 copy-start.21
  491.2 2.9 copy-start.30
  491.2 46.5 %copy-start.7 = (bf16[3,256,768]{2,1,0:T(8,128)(2,1)S(1)}, bf16[3,256,768]{2,1,0:T(8,128)(2,1)}, u32[]{:S(2)}) copy-start(bf16[3,256,768]{2,1,0:T(8,128)(2,1)} %param.16) | copy-start | bytes 3538948
  491.2 46.5 %copy-start.34 = (f32[3,256]{1,0:T(4,128)S(1)}, f32[3,256]{1,0:T(4,128)}, u32[]{:S(2)}) copy-start(f32[3,256]{1,0:T(4,128)} %copy-done.33) | copy-start | bytes 9220
  491.2 46.5 %copy-start.35 = (f32[768]{0:T(1024)S(1)}, f32[768]{0:T(1024)}, u32[]{:S(2)}) copy-start(f32[768]{0:T(1024)} %param.18) | copy-start | bytes 9220
  492.8 47.6 %copy-start.37 = (f32[3,256]{1,0:T(4,128)S(1)}, f32[3,256]{1,0:T(4,128)}, u32[]{:S(2)}) copy-start(f32[3,256]{1,0:T(4,128)} %copy-done.36) | copy-start | bytes 9220
  537.7 2.7 copy-start.12
Sparse Core Ops, SparseCore 0:
  31.9 64.2 all-gather.1
  348.7 139.4 all-reduce.4
  490.7 46.8 reduce-scatter.4
  540.0 47.8 reduce-scatter.2
